TPU v7x, 512 devices: a whole 4x8x8 slice. The times are simulated.
512 devices in a mesh: ctx: 64 (over z_hi, y, core), tp: 8 (over x, z_lo).
Axes of the slice: x: 4, y: 8, z: 8 (z_hi: 4, z_lo: 2; z = z_hi * 2 + z_lo), core: 2. Of those that a mesh axis runs over, the one named last changes fastest.
Arguments:
- query_in: bfloat16 [1024, 16384], P('tp', 'ctx'), may hold values from -6 to 6
- key_in: bfloat16 [1024, 16384], P('tp', 'ctx'), may hold values from -6 to 6
- value_in: bfloat16 [1024, 16384], P('tp', 'ctx'), may hold values from -6 to 6
- short_kernel: float32 [3, 1024, 7], P(None, 'tp'), may hold values from -2 to 2
- basis_weight: float32 [64, 33], replicated, may hold values from -96 to 96
- basis_bias: float32 [64], replicated, may hold values from -3.140625 to 3.140625
- filter_proj: float32 [1024, 64], P('tp'), may hold values from -0.75 to 0.75
- decay_rate: float32 [1024], P('tp'), as said below
- skip_gain: float32 [1024], P('tp'), may hold values from -3 to 3
- grad_out: bfloat16 [1024, 16384], P('tp', 'ctx'), may hold values from -6 to 6
Outputs:
- mixed: bfloat16 [1024, 16384], P('tp', 'ctx')
- grad_query: bfloat16 [1024, 16384], P('tp', 'ctx')
- grad_key: bfloat16 [1024, 16384], P('tp', 'ctx')
- grad_value: bfloat16 [1024, 16384], P('tp', 'ctx')
- grad_proj: float32 [1024, 64], P('tp')
- grad_basis: float32 [64, 33], replicated
Inputs may be any that keep to these rules, and one draw needn't show every extreme that they name: decay_rate is positive in every channel.
All inputs are finite; a program needn't handle non-finite values.
Results may differ from a plain program's by a relative error of at most 0.0066.
Values may be sent and summed in bfloat16 or wider, within the bound.
No kernel may reach another device: no remote copies, remote signals or barrier semaphores. Data moves between devices by JAX's collectives and lax.ppermute only.
A program may use at most 64 MiB of HBM per device.

v0:
```python
import math
import jax
import jax.numpy as jnp
from jax import lax
from jax.sharding import PartitionSpec as P

PRECISE = lax.Precision.HIGHEST


def passed_along(value, axis, steps):
    count = lax.axis_size(axis)
    leading, last = (max(0, -steps), min(count, count - steps))
    return lax.ppermute(value, axis, [(source, source + steps) for source in range(leading, last)])


def features(offset_pos, num_pos, seq_total, num_freq):
    positions = offset_pos + jnp.arange(num_pos, dtype=jnp.int32)
    pieces = [positions.astype(jnp.float32) / seq_total]
    for harmonic in range(1, num_freq + 1):
        angles = (harmonic * positions % seq_total).astype(jnp.float32) * (
            2.0 * math.pi / seq_total
        )
        pieces.append(jnp.cos(angles))
        pieces.append(jnp.sin(angles))
    return jnp.stack(pieces)


def window(decay_rate, offset_pos, num_pos, seq_total):
    positions = (offset_pos + jnp.arange(num_pos, dtype=jnp.int32)).astype(jnp.float32)
    energy = jnp.expm1(-2.0 * decay_rate) / jnp.expm1(-2.0 * decay_rate / seq_total)
    return (
        jnp.exp(-(decay_rate[:, None] * positions[None, :]) / seq_total) / jnp.sqrt(energy)[:, None]
    )


def featurize_rim(signal, before, kernel):
    extended = jnp.concatenate([before, signal], axis=1).astype(jnp.float32)
    num_taps = kernel.shape[1]
    rim_len = num_taps - 1
    num_tok = signal.shape[1]
    result = kernel[:, 0:1] * extended[:, rim_len:]
    for offset in range(1, num_taps):
        result = (
            result
            + kernel[:, offset : offset + 1]
            * extended[:, rim_len - offset : rim_len - offset + num_tok]
        )
    return result


def featurize_back(signal, following, kernel):
    extended = jnp.concatenate([signal, following], axis=1).astype(jnp.float32)
    num_taps = kernel.shape[1]
    num_tok = signal.shape[1]
    result = kernel[:, 0:1] * extended[:, :num_tok]
    for offset in range(1, num_taps):
        result = result + kernel[:, offset : offset + 1] * extended[:, offset : offset + num_tok]
    return result


def tables(num_rows, num_cols, modulus):
    row_ids = jnp.arange(num_rows, dtype=jnp.int32)[:, None]
    col_ids = jnp.arange(num_cols, dtype=jnp.int32)[None, :]
    angles = (row_ids * col_ids % modulus).astype(jnp.float32) * (-2.0 * math.pi / modulus)
    return (jnp.cos(angles), jnp.sin(angles))


def spectrum(signal, outer, twiddle, inner):
    num_chan = signal.shape[0]
    folded = signal.reshape(num_chan, outer[0].shape[1], inner[0].shape[0])
    section_re = jnp.einsum("kt,nts->nks", outer[0], folded, precision=PRECISE)
    section_im = jnp.einsum("kt,nts->nks", outer[1], folded, precision=PRECISE)
    turned_re = section_re * twiddle[0] - section_im * twiddle[1]
    turned_im = section_re * twiddle[1] + section_im * twiddle[0]
    spec_re = jnp.einsum("nks,sj->nkj", turned_re, inner[0], precision=PRECISE) - jnp.einsum(
        "nks,sj->nkj", turned_im, inner[1], precision=PRECISE
    )
    spec_im = jnp.einsum("nks,sj->nkj", turned_re, inner[1], precision=PRECISE) + jnp.einsum(
        "nks,sj->nkj", turned_im, inner[0], precision=PRECISE
    )
    return (spec_re, spec_im)


def restore(spec_re, spec_im, outer, twiddle, inner):
    num_chan = spec_re.shape[0]
    padded_len = outer[0].shape[0] * inner[0].shape[0]
    back_re = jnp.einsum("nkj,sj->nks", spec_re, inner[0], precision=PRECISE) + jnp.einsum(
        "nkj,sj->nks", spec_im, inner[1], precision=PRECISE
    )
    back_im = jnp.einsum("nkj,sj->nks", spec_im, inner[0], precision=PRECISE) - jnp.einsum(
        "nkj,sj->nks", spec_re, inner[1], precision=PRECISE
    )
    turned_re = back_re * twiddle[0] + back_im * twiddle[1]
    turned_im = back_im * twiddle[0] - back_re * twiddle[1]
    result = jnp.einsum("kt,nks->nts", outer[0], turned_re, precision=PRECISE) + jnp.einsum(
        "kt,nks->nts", outer[1], turned_im, precision=PRECISE
    )
    return result.reshape(num_chan, -1) * (1.0 / padded_len)


def convolve_forward(carried_chan, filter_chan, own_skip, transform_tables):
    outer, twiddle, inner = transform_tables
    carried_wide = carried_chan.astype(jnp.float32)
    carried_re, carried_im = spectrum(carried_wide, outer, twiddle, inner)
    filter_re, filter_im = spectrum(filter_chan.astype(jnp.float32), outer, twiddle, inner)
    conv_chan = restore(
        filter_re * carried_re - filter_im * carried_im,
        filter_re * carried_im + filter_im * carried_re,
        outer,
        twiddle,
        inner,
    )
    long_chan = (conv_chan + own_skip[:, None] * carried_wide).astype(jnp.bfloat16)
    return (long_chan, (carried_re, carried_im, filter_re, filter_im))


def convolve_backward(grad_chan, spectra, own_skip, transform_tables):
    outer, twiddle, inner = transform_tables
    carried_re, carried_im, filter_re, filter_im = spectra
    grad_chan_wide = grad_chan.astype(jnp.float32)
    grad_re, grad_im = spectrum(grad_chan_wide, outer, twiddle, inner)
    carried_grad_chan = (
        restore(
            filter_re * grad_re + filter_im * grad_im,
            filter_re * grad_im - filter_im * grad_re,
            outer,
            twiddle,
            inner,
        )
        + own_skip[:, None] * grad_chan_wide
    ).astype(jnp.bfloat16)
    filter_grad_chan = restore(
        carried_re * grad_re + carried_im * grad_im,
        carried_re * grad_im - carried_im * grad_re,
        outer,
        twiddle,
        inner,
    ).astype(jnp.bfloat16)
    return (carried_grad_chan, filter_grad_chan)


def on_device(
    query_in,
    key_in,
    value_in,
    short_kernel,
    basis_weight,
    basis_bias,
    filter_proj,
    decay_rate,
    skip_gain,
    grad_out,
):
    ctx_size = lax.axis_size("ctx")
    ctx_rank = lax.axis_index("ctx")
    tp_size = lax.axis_size("tp")
    num_tok = query_in.shape[1]
    chan_local = query_in.shape[0]
    seq_total = num_tok * ctx_size
    all_channels = chan_local * tp_size
    num_freq = (basis_weight.shape[1] - 1) // 2
    feat_width = basis_weight.shape[0]
    rim_len = short_kernel.shape[2] - 1
    tok_start = ctx_rank * num_tok
    rim_edge = num_tok - rim_len
    per_dev = chan_local // ctx_size
    chan_start = ctx_rank * per_dev
    own_skip = lax.dynamic_slice_in_dim(skip_gain, chan_start, per_dev)
    proj_scale = 1.0 / math.sqrt(seq_total)
    basis_scale = math.sqrt(feat_width / (seq_total * all_channels))
    before = passed_along(
        (query_in[:, rim_edge:], key_in[:, rim_edge:], value_in[:, rim_edge:]), "ctx", 1
    )
    query_feat = featurize_rim(query_in, before[0], short_kernel[0])
    key_feat = featurize_rim(key_in, before[1], short_kernel[1])
    value_feat = featurize_rim(value_in, before[2], short_kernel[2])
    carried = (key_feat * value_feat).astype(jnp.bfloat16)
    grad_wide = grad_out.astype(jnp.float32)
    grad_long = (grad_wide * query_feat).astype(jnp.bfloat16)
    basis_rows = features(tok_start, num_tok, seq_total, num_freq)
    hidden_in = (
        jnp.dot(basis_weight, basis_rows, precision=PRECISE, preferred_element_type=jnp.float32)
        + basis_bias[:, None]
    )
    activation = jnp.sin(hidden_in)
    envelope = window(decay_rate, tok_start, num_tok, seq_total)
    filter_tok = (
        jnp.dot(filter_proj, activation, precision=PRECISE, preferred_element_type=jnp.float32)
        * envelope
    ).astype(jnp.bfloat16)
    inner_len = 2 * ctx_size
    transform_tables = (
        tables(num_tok, num_tok // 2, num_tok),
        tables(num_tok, inner_len, 2 * seq_total),
        tables(inner_len, inner_len, inner_len),
    )
    spread = (
        lax.all_to_all(carried, "ctx", split_axis=0, concat_axis=1, tiled=True),
        lax.all_to_all(filter_tok, "ctx", split_axis=0, concat_axis=1, tiled=True),
    )
    carried_chan = spread[0]
    filter_chan = spread[1]
    long_chan, spectra = convolve_forward(carried_chan, filter_chan, own_skip, transform_tables)
    long_tok = lax.all_to_all(long_chan, "ctx", split_axis=1, concat_axis=0, tiled=True)
    grad_chan = lax.all_to_all(grad_long, "ctx", split_axis=0, concat_axis=1, tiled=True)
    carried_grad_chan, filter_grad_chan = convolve_backward(
        grad_chan, spectra, own_skip, transform_tables
    )
    returned = (
        lax.all_to_all(carried_grad_chan, "ctx", split_axis=1, concat_axis=0, tiled=True),
        lax.all_to_all(filter_grad_chan, "ctx", split_axis=1, concat_axis=0, tiled=True),
    )
    carried_grad = returned[0]
    filter_grad_tok = returned[1]
    long_wide = long_tok.astype(jnp.float32)
    mixed = (query_feat * long_wide).astype(jnp.bfloat16)
    grad_query_feat = (grad_wide * long_wide).astype(jnp.bfloat16)
    grad_raw = filter_grad_tok.astype(jnp.float32) * envelope
    part_proj = jnp.dot(
        grad_raw, activation.T, precision=PRECISE, preferred_element_type=jnp.float32
    )
    grad_hidden = jnp.dot(
        filter_proj.T, grad_raw, precision=PRECISE, preferred_element_type=jnp.float32
    ) * jnp.cos(hidden_in)
    part_basis = jnp.dot(
        grad_hidden, basis_rows.T, precision=PRECISE, preferred_element_type=jnp.float32
    )
    grad_proj = lax.psum(part_proj, "ctx") * proj_scale
    grad_basis = lax.psum(part_basis, ("ctx", "tp")) * basis_scale
    carried_grad_wide = carried_grad.astype(jnp.float32)
    grad_key_feat = (carried_grad_wide * value_feat).astype(jnp.bfloat16)
    grad_value_feat = (carried_grad_wide * key_feat).astype(jnp.bfloat16)
    following = passed_along(
        (grad_query_feat[:, :rim_len], grad_key_feat[:, :rim_len], grad_value_feat[:, :rim_len]),
        "ctx",
        -1,
    )
    grad_query = featurize_back(grad_query_feat, following[0], short_kernel[0]).astype(jnp.bfloat16)
    grad_key = featurize_back(grad_key_feat, following[1], short_kernel[1]).astype(jnp.bfloat16)
    grad_value = featurize_back(grad_value_feat, following[2], short_kernel[2]).astype(jnp.bfloat16)
    return (mixed, grad_query, grad_key, grad_value, grad_proj, grad_basis)


def solution(mesh):
    return jax.shard_map(
        on_device,
        mesh=mesh,
        in_specs=(
            P("tp", "ctx"),
            P("tp", "ctx"),
            P("tp", "ctx"),
            P(None, "tp", None),
            P(),
            P(),
            P("tp", None),
            P("tp"),
            P("tp"),
            P("tp", "ctx"),
        ),
        out_specs=(
            P("tp", "ctx"),
            P("tp", "ctx"),
            P("tp", "ctx"),
            P("tp", "ctx"),
            P("tp", None),
            P(),
        ),
        check_vma=False,
    )
```

profile of v0, /device:TPU:1, one launch (start us, length us, event | category | flops | bytes accessed | tf_op | source)
XLA Modules:
  0.0 538.5 jit_solution(8369667688324918726)
XLA Ops:
  0.6 0.8 slice.242
  1.5 4.6 collective-permute-start
  10.4 15.5 %all-to-all-start = ((bf16[64,2,256]{2,1,0:T(2,128)(2,1)}), bf16[64,2,256]{2,1,0:T(2,128)(2,1)S(1)}, u32[]{:S(2)}, u32[]{:S(2)}) async-start(bf16[64,2,256]{2,1,0:T(2,128)(2,1)} %all_to_all.60), calls=%async_computation | async-start | bytes 131072 | tf_op jit(solution)/shard_map/all_to_all | solution.py:199
  26.0 3.5 collective-permute-start.2
  29.6 2.2 collective-permute-start.1
  35.7 2.4 all-to-all-done
  38.1 9.7 %all-to-all-start.3 = ((bf16[64,2,256]{2,1,0:T(2,128)(2,1)}), bf16[64,2,256]{2,1,0:T(2,128)(2,1)S(1)}, u32[]{:S(2)}, u32[]{:S(2)}) async-start(bf16[64,2,256]{2,1,0:T(2,128)(2,1)} %all_to_all.67), calls=%async_computation.3 | async-start | bytes 131072 | tf_op jit(solution)/shard_map/all_to_all | solution.py:205
  47.8 0.8 convolution_bitcast_fusion.4
  48.6 0.8 convolution_bitcast_fusion.5
  49.4 0.8 fusion.144
  50.1 0.8 convolution_subtract_fusion.5
  50.9 0.8 fusion.121
  51.7 7.9 %all-to-all-done.3 = bf16[64,2,256]{2,1,0:T(2,128)(2,1)S(1)} async-done(((bf16[64,2,256]{2,1,0:T(2,128)(2,1)}), bf16[64,2,256]{2,1,0:T(2,128)(2,1)S(1)}, u32[]{:S(2)}, u32[]{:S(2)}) %all-to-all-start.3) | async-done | bytes 65568 | tf_op jit(solution)/shard_map/all_to_all | solution.py:205
  59.6 0.8 convolution_bitcast_fusion
  60.4 0.8 convolution_bitcast_fusion.1
  61.2 0.8 fusion.134
  62.0 0.8 fusion.114
  62.7 0.8 convolution_subtract_fusion.2
  63.5 0.8 convolution_add_fusion.2
  64.3 0.8 multiply_add_fusion.1
  67.6 11.5 %fusion.19 = f32[2,128,128]{2,1,0:T(8,128)S(1)} fusion(f32[2,256,128]{1,2,0:T(8,128)S(1)} %convolution_subtract_fusion.1, f32[2,256,128]{1,2,0:T(8,128)S(1)} %convolution_add_fusion.1, f32[256,128]{0,1:T(8,128)S(1)} %copy.206, f32[256,128]{0,1:T(8,128)S(1)} %copy.204), kind=kOutput, calls=%fused_computation.45 | convolution fusion | flops 101318656 | bytes 917504 | tf_op jit(solution)/shard_map/kt,nks->nts/dot_general | solution.py:95
  79.1 0.9 fusion.2
  80.9 4.8 all-to-all-start.4
  86.0 12.0 %all-to-all-done.4 = bf16[2,64,256]{2,0,1:T(2,128)(2,1)S(1)} async-done(((bf16[2,64,256]{2,0,1:T(2,128)(2,1)}), bf16[2,64,256]{2,0,1:T(2,128)(2,1)S(1)}, u32[]{:S(2)}, u32[]{:S(2)}) %all-to-all-start.4) | async-done | bytes 65568 | tf_op jit(solution)/shard_map/all_to_all | solution.py:210
  98.5 2.3 collective-permute-start.5
  101.9 6.0 %all-to-all-start.1 = ((bf16[64,2,256]{2,1,0:T(2,128)(2,1)}), bf16[64,2,256]{2,1,0:T(2,128)(2,1)S(1)}, u32[]{:S(2)}, u32[]{:S(2)}) async-start(bf16[64,2,256]{2,1,0:T(2,128)(2,1)} %all_to_all.63), calls=%async_computation.1 | async-start | bytes 131072 | tf_op jit(solution)/shard_map/all_to_all | solution.py:198
  108.0 2.4 collective-permute-start.4
  110.4 1.0 fusion.37
  111.4 2.1 collective-permute-done.4
  113.5 1.0 fusion.44
  114.5 5.6 %all-to-all-done.1 = bf16[64,2,256]{2,1,0:T(2,128)(2,1)S(1)} async-done(((bf16[64,2,256]{2,1,0:T(2,128)(2,1)}), bf16[64,2,256]{2,1,0:T(2,128)(2,1)S(1)}, u32[]{:S(2)}, u32[]{:S(2)}) %all-to-all-start.1) | async-done | bytes 65568 | tf_op jit(solution)/shard_map/all_to_all | solution.py:198
  120.2 0.8 convolution_bitcast_fusion.2
  121.0 0.8 convolution_bitcast_fusion.3
  121.8 0.8 fusion.119
  122.5 0.8 fusion.142
  123.3 0.8 convolution_subtract_fusion.4
  124.0 0.8 multiply_add_fusion
  127.4 0.9 fusion.12
  128.3 0.9 fusion.8
  130.0 7.0 %all-to-all-start.5 = ((bf16[2,64,256]{2,0,1:T(2,128)(2,1)}), bf16[2,64,256]{2,0,1:T(2,128)(2,1)S(1)}, u32[]{:S(2)}, u32[]{:S(2)}) async-start(bf16[2,64,256]{2,0,1:T(2,128)(2,1)} %copy.242), calls=%async_computation.5 | async-start | bytes 131072 | tf_op jit(solution)/shard_map/all_to_all | solution.py:211
  139.6 0.9 fusion.26
  140.5 0.9 fusion.4
  142.3 6.9 %all-to-all-done.5 = bf16[2,64,256]{2,0,1:T(2,128)(2,1)S(1)} async-done(((bf16[2,64,256]{2,0,1:T(2,128)(2,1)}), bf16[2,64,256]{2,0,1:T(2,128)(2,1)S(1)}, u32[]{:S(2)}, u32[]{:S(2)}) %all-to-all-start.5) | async-done | bytes 65568 | tf_op jit(solution)/shard_map/all_to_all | solution.py:211
  149.2 5.8 %all-to-all-start.2 = ((bf16[2,64,256]{2,0,1:T(2,128)(2,1)}), bf16[2,64,256]{2,0,1:T(2,128)(2,1)S(1)}, u32[]{:S(2)}, u32[]{:S(2)}) async-start(bf16[2,64,256]{2,0,1:T(2,128)(2,1)} %copy.223), calls=%async_computation.2 | async-start | bytes 131072 | tf_op jit(solution)/shard_map/all_to_all | solution.py:204
  156.2 99.6 %psum.15 = f32[64,33]{0,1:T(8,128)S(1)} all-reduce(f32[64,33]{0,1:T(8,128)S(1)} %fusion.423), channel_id=1, replica_groups=mesh['ctx'=64,'tp'=8] {'ctx','tp'}, use_global_device_ids=true, to_apply=%region_1.2 | all-reduce | flops 2112 | bytes 16896 | tf_op jit(solution)/shard_map/psum | solution.py:229
  255.8 270.7 %psum.14 = f32[128,64]{0,1:T(8,128)S(1)} all-reduce(f32[128,64]{0,1:T(8,128)S(1)} %fusion.417), channel_id=1, replica_groups=mesh['ctx'=64,'tp'=8] {'ctx'}, use_global_device_ids=true, to_apply=%region_0.1 | all-reduce | flops 8192 | bytes 65536 | tf_op jit(solution)/shard_map/psum | solution.py:228
  528.0 8.4 %collective-permute-start.3 = (bf16[128,6]{1,0:T(8,128)(2,1)S(1)}, bf16[128,6]{1,0:T(8,128)(2,1)S(1)}, u32[]{:S(2)}, u32[]{:S(2)}) collective-permute-start(bf16[128,6]{1,0:T(8,128)(2,1)S(1)} %slice.333), channel_id=1, source_target_pairs={{8,0},{16,8},{24,16},{32,24},{40,32},{48,40},{56,48},{64,56},{72,6... | collective-permute-start | bytes 4616 | tf_op jit(solution)/shard_map/ppermute | solution.py:13
  537.3 1.0 fusion.51
  (116 shorter events, 23.9 us)
Async XLA Ops:
  0.6 8.8 %copy-start = (f32[128,64]{0,1:T(8,128)S(1)}, f32[128,64]{0,1:T(8,128)}, u32[]{:S(2)}) copy-start(f32[128,64]{0,1:T(8,128)} %param.16) | copy-start | bytes 98308
  1.5 32.3 %collective-permute-start = (bf16[128,6]{1,0:T(8,128)(2,1)S(1)}, bf16[128,6]{1,0:T(8,128)(2,1)S(1)}, u32[]{:S(2)}, u32[]{:S(2)}) collective-permute-start(bf16[128,6]{1,0:T(8,128)(2,1)S(1)} %slice.242), channel_id=1, source_target_pairs={{0,8},{8,16},{16,24},{24,32},{32,40},{40,48},{48,56},{56,64},{64,7... | collective-permute-start | bytes 4616 | tf_op jit(solution)/shard_map/ppermute | solution.py:13
  7.5 0.7 copy-start.9
  8.2 0.7 copy-start.5
  8.2 0.7 copy-start.7
  10.4 15.5 %copy-start.3 = (bf16[128,256]{1,0:T(8,128)(2,1)S(1)}, bf16[128,256]{1,0:T(8,128)(2,1)}, u32[]{:S(2)}) copy-start(bf16[128,256]{1,0:T(8,128)(2,1)} %param.12) | copy-start | bytes 196612
  10.4 27.7 %all-to-all-start = ((bf16[64,2,256]{2,1,0:T(2,128)(2,1)}), bf16[64,2,256]{2,1,0:T(2,128)(2,1)S(1)}, u32[]{:S(2)}, u32[]{:S(2)}) async-start(bf16[64,2,256]{2,1,0:T(2,128)(2,1)} %all_to_all.60), calls=%async_computation | async-start | bytes 131072 | tf_op jit(solution)/shard_map/all_to_all | solution.py:199
  25.9 3.6 copy-start.4
  26.0 59.8 %collective-permute-start.2 = (bf16[128,6]{1,0:T(8,128)(2,1)S(1)}, bf16[128,6]{1,0:T(8,128)(2,1)S(1)}, u32[]{:S(2)}, u32[]{:S(2)}) collective-permute-start(bf16[128,6]{1,0:T(8,128)(2,1)S(1)} %slice.274), channel_id=1, source_target_pairs={{0,8},{8,16},{16,24},{24,32},{32,40},{40,48},{48,56},{56,64},{64,7... | collective-permute-start | bytes 4616 | tf_op jit(solution)/shard_map/ppermute | solution.py:13
  29.6 2.7 copy-start.6
  29.6 56.3 %collective-permute-start.1 = (bf16[128,6]{1,0:T(8,128)(2,1)S(1)}, bf16[128,6]{1,0:T(8,128)(2,1)S(1)}, u32[]{:S(2)}, u32[]{:S(2)}) collective-permute-start(bf16[128,6]{1,0:T(8,128)(2,1)S(1)} %slice.258), channel_id=1, source_target_pairs={{0,8},{8,16},{16,24},{24,32},{32,40},{40,48},{48,56},{56,64},{64,7... | collective-permute-start | bytes 4616 | tf_op jit(solution)/shard_map/ppermute | solution.py:13
  33.0 0.9 copy-start.2
  33.1 0.7 copy-start.8
  33.8 0.8 copy-start.1
  38.1 21.5 %all-to-all-start.3 = ((bf16[64,2,256]{2,1,0:T(2,128)(2,1)}), bf16[64,2,256]{2,1,0:T(2,128)(2,1)S(1)}, u32[]{:S(2)}, u32[]{:S(2)}) async-start(bf16[64,2,256]{2,1,0:T(2,128)(2,1)} %all_to_all.67), calls=%async_computation.3 | async-start | bytes 131072 | tf_op jit(solution)/shard_map/all_to_all | solution.py:205
  80.9 17.0 %all-to-all-start.4 = ((bf16[2,64,256]{2,0,1:T(2,128)(2,1)}), bf16[2,64,256]{2,0,1:T(2,128)(2,1)S(1)}, u32[]{:S(2)}, u32[]{:S(2)}) async-start(bf16[2,64,256]{2,0,1:T(2,128)(2,1)} %copy.236), calls=%async_computation.4 | async-start | bytes 131072 | tf_op jit(solution)/shard_map/all_to_all | solution.py:210
  98.5 11.8 %collective-permute-start.5 = (bf16[128,6]{1,0:T(8,128)(2,1)S(1)}, bf16[128,6]{1,0:T(8,128)(2,1)S(1)}, u32[]{:S(2)}, u32[]{:S(2)}) collective-permute-start(bf16[128,6]{1,0:T(8,128)(2,1)S(1)} %slice.349), channel_id=1, source_target_pairs={{8,0},{16,8},{24,16},{32,24},{40,32},{48,40},{56,48},{64,56},{72,6... | collective-permute-start | bytes 4616 | tf_op jit(solution)/shard_map/ppermute | solution.py:13
  101.9 18.2 %all-to-all-start.1 = ((bf16[64,2,256]{2,1,0:T(2,128)(2,1)}), bf16[64,2,256]{2,1,0:T(2,128)(2,1)S(1)}, u32[]{:S(2)}, u32[]{:S(2)}) async-start(bf16[64,2,256]{2,1,0:T(2,128)(2,1)} %all_to_all.63), calls=%async_computation.1 | async-start | bytes 131072 | tf_op jit(solution)/shard_map/all_to_all | solution.py:198
  108.0 5.5 %collective-permute-start.4 = (bf16[128,6]{1,0:T(8,128)(2,1)S(1)}, bf16[128,6]{1,0:T(8,128)(2,1)S(1)}, u32[]{:S(2)}, u32[]{:S(2)}) collective-permute-start(bf16[128,6]{1,0:T(8,128)(2,1)S(1)} %slice.341), channel_id=1, source_target_pairs={{8,0},{16,8},{24,16},{32,24},{40,32},{48,40},{56,48},{64,56},{72,6... | collective-permute-start | bytes 4616 | tf_op jit(solution)/shard_map/ppermute | solution.py:13
  130.0 19.1 %all-to-all-start.5 = ((bf16[2,64,256]{2,0,1:T(2,128)(2,1)}), bf16[2,64,256]{2,0,1:T(2,128)(2,1)S(1)}, u32[]{:S(2)}, u32[]{:S(2)}) async-start(bf16[2,64,256]{2,0,1:T(2,128)(2,1)} %copy.242), calls=%async_computation.5 | async-start | bytes 131072 | tf_op jit(solution)/shard_map/all_to_all | solution.py:211
  149.2 378.0 %all-to-all-start.2 = ((bf16[2,64,256]{2,0,1:T(2,128)(2,1)}), bf16[2,64,256]{2,0,1:T(2,128)(2,1)S(1)}, u32[]{:S(2)}, u32[]{:S(2)}) async-start(bf16[2,64,256]{2,0,1:T(2,128)(2,1)} %copy.223), calls=%async_computation.2 | async-start | bytes 131072 | tf_op jit(solution)/shard_map/all_to_all | solution.py:204
  528.0 9.3 %collective-permute-start.3 = (bf16[128,6]{1,0:T(8,128)(2,1)S(1)}, bf16[128,6]{1,0:T(8,128)(2,1)S(1)}, u32[]{:S(2)}, u32[]{:S(2)}) collective-permute-start(bf16[128,6]{1,0:T(8,128)(2,1)S(1)} %slice.333), channel_id=1, source_target_pairs={{8,0},{16,8},{24,16},{32,24},{40,32},{48,40},{56,48},{64,56},{72,6... | collective-permute-start | bytes 4616 | tf_op jit(solution)/shard_map/ppermute | solution.py:13
where the time goes:
time: 544 us; the launch traced here: 539 us
  blocking collectives  370 us (68%)
  starting transfers between devices  72.2 us (13%)
  matrix products  39.1 us (7%)
  waiting for transfers between devices  37.1 us (7%)
  other arithmetic  9.16 us (2%)
  local copies, waits for them, and re-layouts  8.96 us (2%)
    psum x1, blocking collectives, on_device(): grad_proj = lax.psum(part_proj, 'ctx') * proj_scale  271 us
    psum x1, blocking collectives, on_device(): grad_basis = lax.psum(part_basis, ('ctx', 'tp')) * basis_scale  99.6 us
    ppermute x6, starting transfers between devices, passed_along(): lax.ppermute(value, axis, [(source, source + steps) for source in range(l...  23.4 us
    all_to_all x1, starting transfers between devices, on_device(): lax.all_to_all(filter_tok, 'ctx', split_axis=0, concat_axis=1, tiled=True)  15.5 us
    dot_general x3, matrix products, restore(): jnp.einsum('kt,nks->nts', outer[0], turned_re, precision=PRECISE)  13.3 us
    all_to_all x1, waiting for transfers between devices, on_device(): lax.all_to_all(carried_grad_chan, 'ctx', split_axis=1, concat_axis=0, til...  12 us
  transfers between devices with their start and end apart: 12, of which 7 were waited for; matrix products, arithmetic and copies ran while one was open for 7% of the time, Pallas kernels for 0%

commit v1 on v0

--- a/solution.py
+++ b/solution.py
@@ -225,7 +225,7 @@
     part_basis = jnp.dot(
         grad_hidden, basis_rows.T, precision=PRECISE, preferred_element_type=jnp.float32
     )
-    grad_proj = lax.psum(part_proj, "ctx") * proj_scale
+    grad_proj = jnp.sum(lax.all_gather(part_proj, "ctx"), axis=0) * proj_scale
     grad_basis = lax.psum(part_basis, ("ctx", "tp")) * basis_scale
     carried_grad_wide = carried_grad.astype(jnp.float32)
     grad_key_feat = (carried_grad_wide * value_feat).astype(jnp.bfloat16)

time: 544 us -> 289 us (0.53)
  blocking collectives: 370 us -> 129 us
  starting transfers between devices: 72.2 us -> 54.7 us
  between operations: 1.74 us -> 15.1 us
  matrix products: 39.1 us -> 30.6 us
    psum x1 -> x0, blocking collectives: 271 us -> none  [on_device(): grad_proj = lax.psum(part_proj, 'ctx') * proj_scale]
    all_to_all x0 -> x2, blocking collectives: none -> 31.9 us  [the longest x1 15.9 us: on_device(): lax.all_to_all(filter_grad_chan, 'ctx', split_axis=1, concat_axis=0, tile...]
    all_to_all x2 -> x0, starting transfers between devices: 12.9 us -> none  [the longest x1 6.95 us: on_device(): lax.all_to_all(filter_grad_chan, 'ctx', split_axis=1, concat_axis=0, tile...]
    all_to_all x2 -> x0, waiting for transfers between devices: 12.5 us -> none  [the longest x1 6.9 us: on_device(): lax.all_to_all(filter_grad_chan, 'ctx', split_axis=1, concat_axis=0, tile...]
    all_to_all x1, waiting for transfers between devices: 0.01 us -> 11.1 us  [on_device(): lax.all_to_all(long_chan, 'ctx', split_axis=1, concat_axis=0, tiled=True)]
    dot_general x3, matrix products: 13.3 us -> 2.78 us  [restore(): jnp.einsum('kt,nks->nts', outer[0], turned_re, precision=PRECISE)]
    ppermute x6, starting transfers between devices: 23.4 us -> 16.9 us  [passed_along(): lax.ppermute(value, axis, [(source, source + steps) for source in range(l...]
  transfers between devices with their start and end apart: 12 -> 11, of which waited for: 7 -> 6; matrix products, arithmetic and copies ran while one was open for 7% -> 12% of each run, Pallas kernels for 0% -> 0%
where the time goes in v1:
time: 289 us; the launch traced here: 284 us
  blocking collectives  129 us (45%)
  starting transfers between devices  54.7 us (19%)
  waiting for transfers between devices  35.6 us (12%)
  matrix products  30.6 us (11%)
  between operations  15.1 us (5%)
  other arithmetic  9.97 us (3%)
  local copies, waits for them, and re-layouts  9.34 us (3%)
    psum x1, blocking collectives, on_device(): grad_basis = lax.psum(part_basis, ('ctx', 'tp')) * basis_scale  96.7 us
    ppermute x6, starting transfers between devices, passed_along(): lax.ppermute(value, axis, [(source, source + steps) for source in range(l...  16.9 us
    all_to_all x1, blocking collectives, on_device(): lax.all_to_all(filter_grad_chan, 'ctx', split_axis=1, concat_axis=0, tile...  15.9 us
    all_to_all x1, blocking collectives, on_device(): lax.all_to_all(carried, 'ctx', split_axis=0, concat_axis=1, tiled=True)  15.9 us
    all_to_all x1, starting transfers between devices, on_device(): lax.all_to_all(filter_tok, 'ctx', split_axis=0, concat_axis=1, tiled=True)  15.3 us
    all_to_all x1, waiting for transfers between devices, on_device(): lax.all_to_all(carried_grad_chan, 'ctx', split_axis=1, concat_axis=0, til...  11.9 us
    all_to_all x1, waiting for transfers between devices, on_device(): lax.all_to_all(long_chan, 'ctx', split_axis=1, concat_axis=0, tiled=True)  11.1 us
    all_to_all x1, starting transfers between devices, on_device(): lax.all_to_all(grad_long, 'ctx', split_axis=0, concat_axis=1, tiled=True)  10.4 us
  transfers between devices with their start and end apart: 11, of which 6 were waited for; matrix products, arithmetic and copies ran while one was open for 12% of the time, Pallas kernels for 0%

profile of v1, /device:TPU:1, one launch (start us, length us, event | category | flops | bytes accessed | tf_op | source)
XLA Modules:
  0.0 283.8 jit_solution(11574025529743215977)
XLA Ops:
  7.2 0.9 slice.242
  8.1 4.6 %collective-permute-start = (bf16[128,6]{1,0:T(8,128)(2,1)S(1)}, bf16[128,6]{1,0:T(8,128)(2,1)S(1)}, u32[]{:S(2)}, u32[]{:S(2)}) collective-permute-start(bf16[128,6]{1,0:T(8,128)(2,1)S(1)} %slice.242), channel_id=1, source_target_pairs={{0,8},{8,16},{16,24},{24,32},{32,40},{40,48},{48,56},{56,64},{64,7... | collective-permute-start | bytes 4616 | tf_op jit(solution)/shard_map/ppermute | solution.py:13
  14.9 1.2 fusion.422
  16.2 1.0 fusion.7
  17.8 15.3 %all-to-all-start = ((bf16[64,2,256]{2,1,0:T(2,128)(2,1)}), bf16[64,2,256]{2,1,0:T(2,128)(2,1)S(1)}, u32[]{:S(2)}, u32[]{:S(2)}) async-start(bf16[64,2,256]{2,1,0:T(2,128)(2,1)} %all_to_all.60), calls=%async_computation | async-start | bytes 131072 | tf_op jit(solution)/shard_map/all_to_all | solution.py:199
  33.1 0.8 slice.258
  34.0 3.5 %collective-permute-start.1 = (bf16[128,6]{1,0:T(8,128)(2,1)S(1)}, bf16[128,6]{1,0:T(8,128)(2,1)S(1)}, u32[]{:S(2)}, u32[]{:S(2)}) collective-permute-start(bf16[128,6]{1,0:T(8,128)(2,1)S(1)} %slice.258), channel_id=1, source_target_pairs={{0,8},{8,16},{16,24},{24,32},{32,40},{40,48},{48,56},{56,64},{64,7... | collective-permute-start | bytes 4616 | tf_op jit(solution)/shard_map/ppermute | solution.py:13
  37.5 0.8 slice.274
  38.4 2.0 collective-permute-start.2
  43.6 1.7 all-to-all-done
  45.3 10.4 %all-to-all-start.3 = ((bf16[64,2,256]{2,1,0:T(2,128)(2,1)}), bf16[64,2,256]{2,1,0:T(2,128)(2,1)S(1)}, u32[]{:S(2)}, u32[]{:S(2)}) async-start(bf16[64,2,256]{2,1,0:T(2,128)(2,1)} %all_to_all.67), calls=%async_computation.3 | async-start | bytes 131072 | tf_op jit(solution)/shard_map/all_to_all | solution.py:205
  55.8 0.8 convolution_bitcast_fusion.4
  56.6 0.8 convolution_bitcast_fusion.5
  57.4 0.8 fusion.144
  59.7 7.8 %all-to-all-done.3 = bf16[64,2,256]{2,1,0:T(2,128)(2,1)S(1)} async-done(((bf16[64,2,256]{2,1,0:T(2,128)(2,1)}), bf16[64,2,256]{2,1,0:T(2,128)(2,1)S(1)}, u32[]{:S(2)}, u32[]{:S(2)}) %all-to-all-start.3) | async-done | bytes 65568 | tf_op jit(solution)/shard_map/all_to_all | solution.py:205
  67.5 0.8 convolution_bitcast_fusion
  68.3 0.8 convolution_bitcast_fusion.1
  69.1 0.8 fusion.114
  69.9 0.8 fusion.134
  70.6 0.8 convolution_add_fusion.2
  71.4 0.8 convolution_subtract_fusion.2
  72.2 0.8 multiply_add_fusion.1
  75.5 1.0 fusion.19
  76.6 0.9 fusion.2
  78.4 4.9 %all-to-all-start.4 = ((bf16[2,64,256]{2,0,1:T(2,128)(2,1)}), bf16[2,64,256]{2,0,1:T(2,128)(2,1)S(1)}, u32[]{:S(2)}, u32[]{:S(2)}) async-start(bf16[2,64,256]{2,0,1:T(2,128)(2,1)} %copy.236), calls=%async_computation.4 | async-start | bytes 131072 | tf_op jit(solution)/shard_map/all_to_all | solution.py:210
  83.6 11.9 %all-to-all-done.4 = bf16[2,64,256]{2,0,1:T(2,128)(2,1)S(1)} async-done(((bf16[2,64,256]{2,0,1:T(2,128)(2,1)}), bf16[2,64,256]{2,0,1:T(2,128)(2,1)S(1)}, u32[]{:S(2)}, u32[]{:S(2)}) %all-to-all-start.4) | async-done | bytes 65568 | tf_op jit(solution)/shard_map/all_to_all | solution.py:210
  96.5 15.9 %all_to_all.78 = bf16[64,2,256]{2,1,0:T(2,128)(2,1)S(1)} all-to-all(bf16[64,2,256]{2,1,0:T(2,128)(2,1)S(1)} %all_to_all.63), channel_id=1, replica_groups=mesh['ctx'=64,'tp'=8] {'ctx'}, dimensions={0} | all-to-all | bytes 131072 | tf_op jit(solution)/shard_map/all_to_all | solution.py:198
  112.5 0.8 convolution_bitcast_fusion.2
  113.3 0.8 convolution_bitcast_fusion.3
  116.4 0.8 multiply_add_fusion
  119.8 0.9 fusion.12
  120.6 0.9 fusion.8
  121.8 15.9 %all_to_all.79 = bf16[2,64,256]{2,0,1:T(2,128)(2,1)S(1)} all-to-all(bf16[2,64,256]{2,0,1:T(2,128)(2,1)S(1)} %copy.242), channel_id=1, replica_groups=mesh['ctx'=64,'tp'=8] {'ctx'}, dimensions={1} | all-to-all | bytes 131072 | tf_op jit(solution)/shard_map/all_to_all | solution.py:211
  137.9 1.0 fusion.417
  138.9 2.3 collective-permute-start.4
  141.2 2.1 collective-permute-start.5
  143.3 0.8 collective-permute-done.4
  144.1 2.3 collective-permute-done.5
  146.5 1.0 fusion.44
  150.1 0.9 fusion.26
  150.9 0.9 fusion.4
  152.7 7.0 %all-to-all-start.2 = ((bf16[2,64,256]{2,0,1:T(2,128)(2,1)}), bf16[2,64,256]{2,0,1:T(2,128)(2,1)S(1)}, u32[]{:S(2)}, u32[]{:S(2)}) async-start(bf16[2,64,256]{2,0,1:T(2,128)(2,1)} %copy.223), calls=%async_computation.2 | async-start | bytes 131072 | tf_op jit(solution)/shard_map/all_to_all | solution.py:204
  159.8 1.0 fusion.37
  160.8 11.1 %all-to-all-done.2 = bf16[2,64,256]{2,0,1:T(2,128)(2,1)S(1)} async-done(((bf16[2,64,256]{2,0,1:T(2,128)(2,1)}), bf16[2,64,256]{2,0,1:T(2,128)(2,1)S(1)}, u32[]{:S(2)}, u32[]{:S(2)}) %all-to-all-start.2) | async-done | bytes 65568 | tf_op jit(solution)/shard_map/all_to_all | solution.py:204
  172.7 2.3 collective-permute-start.3
  175.7 96.7 %psum.7 = f32[64,33]{0,1:T(8,128)S(1)} all-reduce(f32[64,33]{0,1:T(8,128)S(1)} %fusion.423), channel_id=1, replica_groups=mesh['ctx'=64,'tp'=8] {'ctx','tp'}, use_global_device_ids=true, to_apply=%region_1.2 | all-reduce | flops 2112 | bytes 16896 | tf_op jit(solution)/shard_map/psum | solution.py:229
  273.0 1.0 fusion.51
  274.0 2.0 copy.273
  (112 shorter events, 23.8 us)
Async XLA Ops:
  7.2 9.0 %copy-start = (f32[128,64]{0,1:T(8,128)S(1)}, f32[128,64]{0,1:T(8,128)}, u32[]{:S(2)}) copy-start(f32[128,64]{0,1:T(8,128)} %param.16) | copy-start | bytes 98308
  7.2 35.3 %copy-start.2 = (bf16[128,256]{1,0:T(8,128)(2,1)S(1)}, bf16[128,256]{1,0:T(8,128)(2,1)}, u32[]{:S(2)}) copy-start(bf16[128,256]{1,0:T(8,128)(2,1)} %param.10) | copy-start | bytes 196612
  7.2 35.2 %copy-start.5 = (f32[128]{0:T(128)S(1)}, f32[128]{0:T(128)}, u32[]{:S(2)}) copy-start(f32[128]{0:T(128)} %param.18) | copy-start | bytes 1540
  7.2 35.4 %copy-start.1 = (bf16[128,256]{1,0:T(8,128)(2,1)S(1)}, bf16[128,256]{1,0:T(8,128)(2,1)}, u32[]{:S(2)}) copy-start(bf16[128,256]{1,0:T(8,128)(2,1)} %param.19) | copy-start | bytes 196612
  8.1 34.4 %collective-permute-start = (bf16[128,6]{1,0:T(8,128)(2,1)S(1)}, bf16[128,6]{1,0:T(8,128)(2,1)S(1)}, u32[]{:S(2)}, u32[]{:S(2)}) collective-permute-start(bf16[128,6]{1,0:T(8,128)(2,1)S(1)} %slice.242), channel_id=1, source_target_pairs={{0,8},{8,16},{16,24},{24,32},{32,40},{40,48},{48,56},{56,64},{64,7... | collective-permute-start | bytes 4616 | tf_op jit(solution)/shard_map/ppermute | solution.py:13
  17.8 27.5 %all-to-all-start = ((bf16[64,2,256]{2,1,0:T(2,128)(2,1)}), bf16[64,2,256]{2,1,0:T(2,128)(2,1)S(1)}, u32[]{:S(2)}, u32[]{:S(2)}) async-start(bf16[64,2,256]{2,1,0:T(2,128)(2,1)} %all_to_all.60), calls=%async_computation | async-start | bytes 131072 | tf_op jit(solution)/shard_map/all_to_all | solution.py:199
  34.0 49.4 %collective-permute-start.1 = (bf16[128,6]{1,0:T(8,128)(2,1)S(1)}, bf16[128,6]{1,0:T(8,128)(2,1)S(1)}, u32[]{:S(2)}, u32[]{:S(2)}) collective-permute-start(bf16[128,6]{1,0:T(8,128)(2,1)S(1)} %slice.258), channel_id=1, source_target_pairs={{0,8},{8,16},{16,24},{24,32},{32,40},{40,48},{48,56},{56,64},{64,7... | collective-permute-start | bytes 4616 | tf_op jit(solution)/shard_map/ppermute | solution.py:13
  38.4 45.2 %collective-permute-start.2 = (bf16[128,6]{1,0:T(8,128)(2,1)S(1)}, bf16[128,6]{1,0:T(8,128)(2,1)S(1)}, u32[]{:S(2)}, u32[]{:S(2)}) collective-permute-start(bf16[128,6]{1,0:T(8,128)(2,1)S(1)} %slice.274), channel_id=1, source_target_pairs={{0,8},{8,16},{16,24},{24,32},{32,40},{40,48},{48,56},{56,64},{64,7... | collective-permute-start | bytes 4616 | tf_op jit(solution)/shard_map/ppermute | solution.py:13
  45.3 22.2 %all-to-all-start.3 = ((bf16[64,2,256]{2,1,0:T(2,128)(2,1)}), bf16[64,2,256]{2,1,0:T(2,128)(2,1)S(1)}, u32[]{:S(2)}, u32[]{:S(2)}) async-start(bf16[64,2,256]{2,1,0:T(2,128)(2,1)} %all_to_all.67), calls=%async_computation.3 | async-start | bytes 131072 | tf_op jit(solution)/shard_map/all_to_all | solution.py:205
  74.9 8.5 %copy-start.3 = (bf16[128,256]{1,0:T(8,128)(2,1)S(1)}, bf16[128,256]{1,0:T(8,128)(2,1)}, u32[]{:S(2)}) copy-start(bf16[128,256]{1,0:T(8,128)(2,1)} %param.11) | copy-start | bytes 196612
  74.9 8.6 %copy-start.4 = (bf16[128,256]{1,0:T(8,128)(2,1)S(1)}, bf16[128,256]{1,0:T(8,128)(2,1)}, u32[]{:S(2)}) copy-start(bf16[128,256]{1,0:T(8,128)(2,1)} %param.12) | copy-start | bytes 196612
  78.4 17.1 %all-to-all-start.4 = ((bf16[2,64,256]{2,0,1:T(2,128)(2,1)}), bf16[2,64,256]{2,0,1:T(2,128)(2,1)S(1)}, u32[]{:S(2)}, u32[]{:S(2)}) async-start(bf16[2,64,256]{2,0,1:T(2,128)(2,1)} %copy.236), calls=%async_computation.4 | async-start | bytes 131072 | tf_op jit(solution)/shard_map/all_to_all | solution.py:210
  83.3 190.7 %all-gather.3.cloned.1.call-start = ((), (), s32[]{:S(2)}) async-start(), calls=%async_computation.6 | async-start | bytes 2129920 | tf_op jit(solution)/shard_map/all_gather | solution.py:228
  118.5 19.4 %copy-start.6 = (f32[128]{0:T(128)S(1)}, f32[128]{0:T(128)}, u32[]{:S(2)}) copy-start(f32[128]{0:T(128)} %param.17) | copy-start | bytes 1540
  138.9 5.2 %collective-permute-start.4 = (bf16[128,6]{1,0:T(8,128)(2,1)S(1)}, bf16[128,6]{1,0:T(8,128)(2,1)S(1)}, u32[]{:S(2)}, u32[]{:S(2)}) collective-permute-start(bf16[128,6]{1,0:T(8,128)(2,1)S(1)} %slice.341), channel_id=1, source_target_pairs={{8,0},{16,8},{24,16},{32,24},{40,32},{48,40},{56,48},{64,56},{72,6... | collective-permute-start | bytes 4616 | tf_op jit(solution)/shard_map/ppermute | solution.py:13
  141.2 5.2 %collective-permute-start.5 = (bf16[128,6]{1,0:T(8,128)(2,1)S(1)}, bf16[128,6]{1,0:T(8,128)(2,1)S(1)}, u32[]{:S(2)}, u32[]{:S(2)}) collective-permute-start(bf16[128,6]{1,0:T(8,128)(2,1)S(1)} %slice.349), channel_id=1, source_target_pairs={{8,0},{16,8},{24,16},{32,24},{40,32},{48,40},{56,48},{64,56},{72,6... | collective-permute-start | bytes 4616 | tf_op jit(solution)/shard_map/ppermute | solution.py:13
  152.7 19.2 %all-to-all-start.2 = ((bf16[2,64,256]{2,0,1:T(2,128)(2,1)}), bf16[2,64,256]{2,0,1:T(2,128)(2,1)S(1)}, u32[]{:S(2)}, u32[]{:S(2)}) async-start(bf16[2,64,256]{2,0,1:T(2,128)(2,1)} %copy.223), calls=%async_computation.2 | async-start | bytes 131072 | tf_op jit(solution)/shard_map/all_to_all | solution.py:204
  172.7 100.2 %collective-permute-start.3 = (bf16[128,6]{1,0:T(8,128)(2,1)S(1)}, bf16[128,6]{1,0:T(8,128)(2,1)S(1)}, u32[]{:S(2)}, u32[]{:S(2)}) collective-permute-start(bf16[128,6]{1,0:T(8,128)(2,1)S(1)} %slice.333), channel_id=1, source_target_pairs={{8,0},{16,8},{24,16},{32,24},{40,32},{48,40},{56,48},{64,56},{72,6... | collective-permute-start | bytes 4616 | tf_op jit(solution)/shard_map/ppermute | solution.py:13
Sparse Core Ops, SparseCore 0:
  139.0 75.6 all-gather.2
